TPU v7x, 512 devices: a whole 4x4x16 slice. The times are simulated.
512 devices in a mesh: row: 16 (over x, z_lo), col: 32 (over y, z_hi, core).
Axes of the slice: x: 4, y: 4, z: 16 (z_hi: 4, z_lo: 4; z = z_hi * 4 + z_lo), core: 2. Of those that a mesh axis runs over, the one named last changes fastest.
Arguments:
- features: bfloat16 [65536, 256], P(('col', 'row')), may hold values from -6 to 6
- weight: bfloat16 [256, 256], replicated, may hold values from -0.375 to 0.375
- cotangent: bfloat16 [65536, 256], P(('row', 'col')), may hold values from -6 to 6
- block_index: int32 [16, 32, 32], P('row', 'col'), may hold values from 0 to 511, as said below
- block_count: int32 [16, 32], P('row', 'col'), may hold values from 1 to 32, as said below
- block_values: bfloat16 [16, 32, 32, 128, 128], P('row', 'col'), may hold values from -0.125 to 0.125
Outputs:
- hidden_out: bfloat16 [65536, 256], P(('row', 'col'))
- input_grad: bfloat16 [65536, 256], P(('col', 'row'))
- weight_grad: float32 [256, 256], replicated
Inputs may be any that keep to these rules, and one draw needn't show every extreme that they name: `block_index`: the 32 entries of one tile are distinct; slots at or after the tile's count hold blocks that are not used. `block_count`: at least one tile holds exactly 32 blocks.
All inputs are finite; a program needn't handle non-finite values.
Results may differ from a plain program's by a relative error of at most 0.015.
Values may be sent and summed in bfloat16 or wider, within the bound.
A program may use at most 64 MiB of HBM per device.

v0:
```python
import math

import jax
import jax.numpy as jnp
from jax import lax
from jax.sharding import PartitionSpec as P

GROUP = 32


def forward_tile(blocks_in, values, index, count, rows_out):
    ncols = blocks_in.shape[0]
    size = blocks_in.shape[1]
    width = blocks_in.shape[2]
    lanes = jnp.arange(GROUP, dtype=jnp.int32)
    targets = jnp.arange(rows_out, dtype=jnp.int32)

    def forward_advance(group_id, totals):
        start = (group_id * GROUP).astype(jnp.int32)
        live = start + lanes < count
        picked = jnp.take(blocks_in, index % ncols, axis=0)
        product = jnp.einsum("gij,gjd->gid", values, picked, preferred_element_type=jnp.float32)
        selector = ((index // ncols)[None, :] == targets[:, None]) & live[None, :]
        return totals + jnp.einsum(
            "rg,gid->rid", selector.astype(jnp.float32), product, precision=lax.Precision.HIGHEST
        )

    zeros = jnp.zeros((rows_out, size, width), jnp.float32)
    groups = (count + GROUP - 1) // GROUP
    return lax.fori_loop(jnp.int32(0), groups, forward_advance, zeros)


def backward_tile(blocks_grad, values, index, count, cols_out):
    size = blocks_grad.shape[1]
    width = blocks_grad.shape[2]
    lanes = jnp.arange(GROUP, dtype=jnp.int32)
    targets = jnp.arange(cols_out, dtype=jnp.int32)

    def backward_advance(group_id, totals):
        start = (group_id * GROUP).astype(jnp.int32)
        live = start + lanes < count
        picked = jnp.take(blocks_grad, index // cols_out, axis=0)
        product = jnp.einsum("gij,gid->gjd", values, picked, preferred_element_type=jnp.float32)
        selector = ((index % cols_out)[None, :] == targets[:, None]) & live[None, :]
        return totals + jnp.einsum(
            "cg,gjd->cjd", selector.astype(jnp.float32), product, precision=lax.Precision.HIGHEST
        )

    zeros = jnp.zeros((cols_out, size, width), jnp.float32)
    groups = (count + GROUP - 1) // GROUP
    return lax.fori_loop(jnp.int32(0), groups, backward_advance, zeros)


def body(features, weight, cotangent, block_index, block_count, block_values):
    row_total = lax.axis_size("row")
    col_total = lax.axis_size("col")
    rows = features.shape[0]
    width = features.shape[1]
    size = block_values.shape[-1]
    block_rows = rows * col_total // size
    block_cols = rows * row_total // size
    index = block_index[0, 0]
    count = block_count[0, 0]
    values = block_values[0, 0]
    own_projected = jnp.dot(features, weight, preferred_element_type=jnp.float32).astype(
        jnp.bfloat16
    )
    projected = lax.all_gather(own_projected, "row", axis=0, tiled=True)
    partial_out = forward_tile(
        projected.reshape(block_cols, size, width), values, index, count, block_rows
    )
    summed_out = lax.psum_scatter(
        partial_out.reshape(block_rows * size, width).astype(jnp.bfloat16),
        "col",
        scatter_dimension=0,
        tiled=True,
    )
    grad_rows = lax.all_gather(cotangent, "col", axis=0, tiled=True)
    partial_back = backward_tile(
        grad_rows.reshape(block_rows, size, width), values, index, count, block_cols
    )
    partial_back = partial_back.reshape(block_cols * size, width)
    grad_sum = lax.psum_scatter(
        partial_back.astype(jnp.bfloat16), "row", scatter_dimension=0, tiled=True
    ).astype(jnp.float32)
    input_grad = jnp.dot(
        grad_sum, weight.astype(jnp.float32).T, precision=lax.Precision.HIGHEST
    ).astype(jnp.bfloat16)
    term = jnp.dot(features.astype(jnp.float32).T, grad_sum, precision=lax.Precision.HIGHEST)
    total = lax.psum(term, ("row", "col"))
    nodes = rows * row_total * col_total
    weight_grad = total / math.sqrt(nodes)
    return (summed_out, input_grad, weight_grad)


def solution(mesh):
    in_specs = (
        P(("col", "row"), None),
        P(),
        P(("row", "col"), None),
        P("row", "col", None),
        P("row", "col"),
        P("row", "col", None, None, None),
    )
    out_specs = (P(("row", "col"), None), P(("col", "row"), None), P())
    return jax.shard_map(body, mesh=mesh, in_specs=in_specs, out_specs=out_specs, check_vma=False)
```

profile of v0, /device:TPU:1, one launch (start us, length us, event | category | flops | bytes accessed | tf_op | source)
XLA Modules:
  0.0 880.9 jit_solution(7760522335443745997)
XLA Ops:
  7.2 0.0 copy-start
  7.2 0.0 all-gather.5.cloned.1.call-start
  7.2 0.7 all-gather.5.cloned.1.call-update
  7.9 0.0 reduce-scatter.5.cloned.1.call-start
  8.6 0.7 fusion.42
  9.3 0.7 bitcast_sign_fusion.1
  10.0 85.3 %all-gather.5.cloned.1.call-done = bf16[4096,256]{1,0:T(8,128)(2,1)} async-done(((bf16[128,256]{1,0:T(8,128)(2,1)}), bf16[4096,256]{1,0:T(8,128)(2,1)}) %all-gather.5.cloned.1.call-update) | async-done | bytes 2097168 | tf_op jit(solution)/shard_map/all_gather | solution.py:78
  95.2 3.7 gather_fusion.1
  98.9 0.0 copy-start.4
  98.9 0.2 broadcast_in_dim.63
  99.1 0.4 copy-done.4
  99.5 15.7 %while.34 = (s32[]{:T(128)}, f32[16,128,256]{2,0,1:T(8,128)S(1)}, s32[]{:T(128)}, s32[32]{0:T(128)S(1)}, s32[32]{0:T(128)S(1)}, /*index=5*/s32[]{:T(128)}, s32[3...) while((s32[]{:T(128)}, f32[16,128,256]{2,0,1:T(8,128)S(1)}, ...), condition=%wide.region_4.5_spmd.clone, body=%wide.region_3.4_spmd.clone.sunk | while | flops 471336928 | bytes 24118400 | solution.py:51
  99.5 0.7 compare_and_fusion.4
  100.2 4.6 fusion.69
  104.8 5.5 copy.20
  110.4 4.8 fusion.70
  115.2 0.0 copy-start.2
  115.2 2.1 copy.17
  117.3 0.0 reduce-scatter.5.cloned.1.call-update
  117.4 0.0 all-gather.3.cloned.1.call-start
  117.4 0.0 copy-done
  117.4 0.0 copy-done.2
  117.4 0.8 convolution_convert_fusion.1
  118.2 0.0 all-gather.3.cloned.1.call-update
  118.3 0.0 all-reduce.2.cloned.1.call-start
  118.3 74.3 %reduce-scatter.5.cloned.1.call-done = bf16[128,256]{1,0:T(8,128)(2,1)} async-done(((bf16[2048,256]{1,0:T(8,128)(2,1)}), bf16[128,256]{1,0:T(8,128)(2,1)}) %reduce-scatter.5.cloned.1.call-update) | async-done | bytes 65552 | tf_op jit(solution)/shard_map/reduce_scatter | solution.py:83
  192.6 1.8 convolution_bitcast_fusion
  194.3 0.0 all-reduce.2.cloned.1.call-update
  194.4 0.0 reduce-scatter.3.cloned.1.call-start
  194.4 86.3 %all-gather.3.cloned.1.call-done = bf16[2048,256]{1,0:T(8,128)(2,1)} async-done(((bf16[128,256]{1,0:T(8,128)(2,1)}), bf16[2048,256]{1,0:T(8,128)(2,1)}) %all-gather.3.cloned.1.call-update) | async-done | bytes 1048592 | tf_op jit(solution)/shard_map/all_gather | solution.py:68
  280.7 0.0 copy-start.1
  280.7 2.5 broadcast_in_dim.62
  283.2 0.0 copy-done.1
  283.2 18.6 %while.35 = (s32[]{:T(128)}, f32[32,128,256]{2,0,1:T(8,128)}, s32[]{:T(128)}, s32[1,32]{1,0:T(1,128)S(1)}, s32[32]{0:T(128)S(1)}, /*index=5*/s32[1,32]{1,0:T(1,1...) while((s32[]{:T(128)}, f32[32,128,256]{2,0,1:T(8,128)}, ...), condition=%wide.region_1.2_spmd.clone.clone, body=%wide.region_0.1_spmd.clone.clone.sunk | while | flops 673190272 | bytes 32511760 | solution.py:30
  283.2 0.7 compare_and_fusion.5
  283.9 0.7 gather_fusion
  284.6 4.0 fusion.76
  288.6 5.5 copy.21
  294.1 7.7 fusion.78
  301.8 2.5 convert_element_type.25
  304.3 2.5 copy.11
  306.8 0.0 reduce-scatter.3.cloned.1.call-update
  306.9 0.8 copy-done.3
  307.7 0.8 convolution_convert_fusion
  308.5 442.9 %all-reduce.2.cloned.1.call-done = f32[256,256]{0,1:T(8,128)} async-done(((f32[256,256]{0,1:T(8,128)}), f32[256,256]{0,1:T(8,128)}) %all-reduce.2.cloned.1.call-update) | async-done | bytes 262160 | tf_op jit(solution)/shard_map/psum | solution.py:90
  751.4 1.0 broadcast_multiply_fusion
  752.4 0.8 copy.13
  753.3 121.2 %reduce-scatter.3.cloned.1.call-done = bf16[128,256]{1,0:T(8,128)(2,1)} async-done(((bf16[4096,256]{1,0:T(8,128)(2,1)}), bf16[128,256]{1,0:T(8,128)(2,1)}) %reduce-scatter.3.cloned.1.call-update) | async-done | bytes 65552 | tf_op jit(solution)/shard_map/reduce_scatter | solution.py:72
  (7 shorter events, 0.0 us)
Async XLA Ops:
  7.2 110.2 %copy-start = (bf16[256,256]{1,0:T(8,128)(2,1)S(1)}, bf16[256,256]{1,0:T(8,128)(2,1)}, u32[]{:S(2)}) copy-start(bf16[256,256]{1,0:T(8,128)(2,1)} %param.11) | copy-start | bytes 393220
  7.2 88.0 %all-gather.5.cloned.1.call-start = ((), (), s32[]{:S(2)}) async-start(), calls=%async_computation.4 | async-start | bytes 2162688 | tf_op jit(solution)/shard_map/all_gather | solution.py:78
  7.9 184.7 %reduce-scatter.5.cloned.1.call-start = ((), (), s32[]{:S(2)}) async-start(), calls=%async_computation.5 | async-start | bytes 1114112 | tf_op jit(solution)/shard_map/reduce_scatter | solution.py:83
  98.9 0.7 copy-start.4
  115.2 2.2 copy-start.2
  117.4 163.3 %all-gather.3.cloned.1.call-start = ((), (), s32[]{:S(2)}) async-start(), calls=%async_computation.2 | async-start | bytes 1114112 | tf_op jit(solution)/shard_map/all_gather | solution.py:68
  118.3 633.2 %all-reduce.2.cloned.1.call-start = ((), (), s32[]{:S(2)}) async-start(), calls=%async_computation.6 | async-start | bytes 524288 | tf_op jit(solution)/shard_map/psum | solution.py:90
  194.4 680.1 %reduce-scatter.3.cloned.1.call-start = ((), (), s32[]{:S(2)}) async-start(), calls=%async_computation.3 | async-start | bytes 2162688 | tf_op jit(solution)/shard_map/reduce_scatter | solution.py:72
  280.7 2.5 copy-start.1
  306.8 0.8 copy-start.3
Sparse Core Ops, SparseCore 0:
  11.1 84.0 all-gather.4
  117.5 75.0 reduce-scatter.4
  195.4 85.2 all-gather.2
  287.5 463.9 all-reduce.1
  756.3 118.0 reduce-scatter.2
where the time goes:
time: 882 us; the launch traced here: 881 us
  waiting for transfers between devices  811 us (92%)
  local copies, waits for them, and re-layouts  24.8 us (3%)
  matrix products  24.6 us (3%)
  between operations  14.5 us (2%)
    psum x1, waiting for transfers between devices, body(): total = lax.psum(term, ('row', 'col'))  443 us
    reduce_scatter x1, waiting for transfers between devices, body(): lax.psum_scatter(partial_out.reshape(block_rows * size, width).astype(jnp...  121 us
    all_gather x1, waiting for transfers between devices, body(): projected = lax.all_gather(own_projected, 'row', axis=0, tiled=True)  86.3 us
    all_gather x1, waiting for transfers between devices, body(): grad_rows = lax.all_gather(cotangent, 'col', axis=0, tiled=True)  85.3 us
    reduce_scatter x1, waiting for transfers between devices, body(): lax.psum_scatter(partial_back.astype(jnp.bfloat16), 'row', scatter_dimens...  74.3 us
  transfers between devices with their start and end apart: 5, of which 5 were waited for; matrix products, arithmetic and copies ran while one was open for 4% of the time, Pallas kernels for 0%

commit v1 on v0

v1 whole, which is shorter than its diff:
```python
import functools
import math

import jax
import jax.numpy as jnp
from jax import lax
from jax.experimental import pallas as pl
from jax.experimental.pallas import tpu as pltpu
from jax.sharding import PartitionSpec as P

MESH = pl.DeviceIdType.MESH
BF = jnp.bfloat16
F32 = jnp.float32
RING = 4
ORDER = (2, 1, 3, 0)


def ids():
    table = {}

    def of(*key):
        return table.setdefault(key, len(table))

    return of


COPIES = 128


def kernel(
    feat, weight, cot, idxv, idxs, cnt, vals,
    out_o, ig_o, wg_o,
    fa, ca, proj, run, pout, pback, tbl_v, tbl_s,
    rc, sy, own_y, ry, sz, rz, rx, szl, rzl,
    wacc, w1s, w1r, w1, w2s, w2r, w2, w3r, w4, w5,
    ss, rs, ls,
):
    of = ids()
    row = lax.axis_index("row")
    col = lax.axis_index("col")
    x, zl = row // 4, lax.rem(row, 4)
    y, zh, c = col // 8, lax.rem(col // 2, 4), lax.rem(col, 2)
    sib = 1 - c

    def r4(v):
        return lax.rem(v, 4)

    def dev(x_=x, zl_=zl, y_=y, zh_=zh, c_=c):
        return (x_ * 4 + zl_, y_ * 8 + zh_ * 2 + c_)

    def at(axis, k):
        here = {"x": x, "zl": zl, "y": y, "zh": zh}[axis]
        there = r4(here + k)
        return dev(**{axis + "_": there}), there

    sends = []

    def send(src, dst, key, device):
        n = of(*key)
        copy = pltpu.make_async_remote_copy(
            src_ref=src, dst_ref=dst, send_sem=ss.at[n], recv_sem=rs.at[n],
            device_id=device, device_id_type=MESH,
        )
        copy.start()
        sends.append(copy)

    def arrive(dst, key):
        n = of(*key)
        pltpu.make_async_remote_copy(
            src_ref=dst, dst_ref=dst, send_sem=ss.at[n], recv_sem=rs.at[n],
            device_id=dev(c_=sib), device_id_type=MESH,
        ).wait_recv()

    barrier = pltpu.get_barrier_semaphore()
    partners = [at(a, k)[0] for a in ("x", "zl", "y", "zh") for k in (1, 2, 3)]
    partners.append(dev(c_=sib))
    for p in partners:
        pl.semaphore_signal(barrier, inc=1, device_id=p, device_id_type=MESH)

    fa[row] = feat[...]
    ca[col] = cot[...]

    lane = lax.broadcasted_iota(jnp.int32, (1, 128), 1)
    tbl_v[...] = jnp.zeros_like(tbl_v)
    tbl_v[0:1, 0:32] = idxv[...]
    index = tbl_v[0:1, :]
    srow, scol = index // 16, lax.rem(index, jnp.full_like(index, 16))
    count = cnt[0, 0]
    none = jnp.full((1, 128), 32, jnp.int32)

    def link(t, carry):
        pf, lf, pb, lb = carry
        i = idxs[0, t]
        ti, tj = i // 16, lax.rem(i, 16)
        later = lane > t
        pf = jnp.where(later & (srow == ti), t, pf)
        pb = jnp.where(later & (scol == tj), t, pb)
        live = jnp.full((1, 128), t, jnp.int32) < count
        lf = jnp.where(live & (lane == ti), t, lf)
        lb = jnp.where(live & (lane == tj), t, lb)
        return pf, lf, pb, lb

    pf, lf, pb, lb = lax.fori_loop(0, 32, link, (none, none, none, none))
    tbl_v[0:1, :] = scol
    tbl_v[1:2, :] = pf
    tbl_v[2:3, :] = lf
    tbl_v[3:4, :] = srow
    tbl_v[4:5, :] = pb
    tbl_v[5:6, :] = lb
    table = pltpu.make_async_copy(tbl_v, tbl_s, ls)
    table.start()

    pl.semaphore_wait(barrier, len(partners))

    def features_on(block, tag):
        for k in (1, 2, 3):
            d, _ = at("x", k)
            send(fa.at[block], fa.at[block], ("fx", k, tag), d)

    def cotangents_on(block, tag):
        for k in (1, 2, 3):
            d, _ = at("y", k)
            send(ca.at[block], ca.at[block], ("cy", k, tag), d)
        send(ca.at[block], ca.at[block], ("cs", 0, tag), dev(c_=sib))

    for k in (1, 3, 2):
        send(fa.at[row], fa.at[row], ("fz", k), at("zl", k)[0])
    for k in (1, 3, 2):
        send(ca.at[col], ca.at[col], ("cz", k), at("zh", k)[0])
    features_on(row, 0)
    cotangents_on(col, 0)
    for k in (1, 3, 2):
        block = x * 4 + r4(zl + 4 - k)
        arrive(fa.at[block], ("fz", k))
        features_on(block, k)
    for k in (1, 3, 2):
        block = y * 8 + r4(zh + 4 - k) * 2 + c
        arrive(ca.at[block], ("cz", k))
        cotangents_on(block, k)

    table.wait()
    run[32] = jnp.zeros_like(run[32])

    for tag in (0, 1, 3, 2):
        for k in (1, 3, 2):
            block = r4(x + 4 - k) * 4 + r4(zl + 4 - tag)
            arrive(fa.at[block], ("fx", k, tag))

    def project(j, carry):
        proj[j] = jnp.dot(fa[j], weight[...], preferred_element_type=F32).astype(BF)
        return carry

    lax.fori_loop(0, 16, project, 0)

    def forward(s, carry):
        product = jnp.dot(vals[s], proj[tbl_s[0, s]], preferred_element_type=F32)
        run[s] = product + run[tbl_s[1, s]]
        return carry

    lax.fori_loop(0, 32, forward, 0)

    def forward_out(o, carry):
        r = lax.rem(o, 4) * 8 + lax.rem(o // 4, 4) * 2 + o // 16
        pout[o] = run[tbl_s[2, r]].astype(BF)
        return carry

    lax.fori_loop(0, 32, forward_out, 0)

    def group(g):
        return r4(zh + ORDER[g])

    for g in range(4):
        part = pl.ds(sib * 16 + group(g) * 4, 4)
        send(pout.at[part], rc.at[pl.ds(g * 4, 4)], ("oc", g), dev(c_=sib))

    for tag in (0, 1, 3, 2):
        for k in (1, 3, 2):
            block = r4(y + 4 - k) * 8 + r4(zh + 4 - tag) * 2 + c
            arrive(ca.at[block], ("cy", k, tag))
            send(ca.at[block], ca.at[block], ("cs", k, tag), dev(c_=sib))

    for g in range(4):
        arrive(rc.at[pl.ds(g * 4, 4)], ("oc", g))
        for k in (2, 1, 3):
            d, there = at("y", k)
            own = pout[c * 16 + group(g) * 4 + there].astype(F32)
            sy[g * 3 + k - 1] = (own + rc[g * 4 + there].astype(F32)).astype(BF)
            send(sy.at[g * 3 + k - 1], ry.at[g * 3 + k - 1], ("oy", g, k), d)
        own_y[g] = pout[c * 16 + group(g) * 4 + y].astype(F32) + rc[g * 4 + y].astype(F32)

    for tag in (0, 1, 3, 2):
        for k in (0, 1, 3, 2):
            block = r4(y + 4 - k) * 8 + r4(zh + 4 - tag) * 2 + sib
            arrive(ca.at[block], ("cs", k, tag))

    def backward(s, carry):
        product = lax.dot_general(
            vals[s], ca[tbl_s[3, s]], (((0,), (0,)), ((), ())), preferred_element_type=F32
        )
        run[s] = product + run[tbl_s[4, s]]
        return carry

    lax.fori_loop(0, 32, backward, 0)

    def backward_out(j, carry):
        pback[j] = run[tbl_s[5, j]].astype(BF)
        return carry

    lax.fori_loop(0, 16, backward_out, 0)

    for g in range(4):
        zt = r4(zl + ORDER[g])
        for k in (2, 1, 3):
            d, there = at("x", k)
            send(pback.at[there * 4 + zt], rx.at[g * 3 + k - 1], ("bx", g, k), d)

    wacc[...] = jnp.zeros_like(wacc)

    def weight_term(j, carry):
        wacc[...] += lax.dot_general(
            fa[j], pback[j], (((0,), (0,)), ((), ())), preferred_element_type=F32
        )
        return carry

    lax.fori_loop(0, 16, weight_term, 0)
    w1s[...] = wacc[pl.ds(pl.multiple_of(sib * 128, 128), 128), :].astype(BF)
    send(w1s, w1r, ("w1",), dev(c_=sib))

    def total_y(g):
        total = own_y[g]
        for k in (1, 2, 3):
            arrive(ry.at[g * 3 + k - 1], ("oy", g, k))
            total = total + ry[g * 3 + k - 1].astype(F32)
        return total

    for g in range(3):
        sz[g] = total_y(g).astype(BF)
        send(sz.at[g], rz.at[g], ("oz", g), at("zh", ORDER[g])[0])

    arrive(w1r, ("w1",))
    w1[...] = wacc[pl.ds(pl.multiple_of(c * 128, 128), 128), :] + w1r[...].astype(F32)
    for k in (2, 1, 3):
        d, there = at("x", k)
        w2s[k - 1] = w1[pl.ds(pl.multiple_of(there * 32, 32), 32), :].astype(BF)
        send(w2s.at[k - 1], w2r.at[k - 1], ("w2", k), d)

    def total_x(g):
        total = pback[x * 4 + r4(zl + ORDER[g])].astype(F32)
        for k in (1, 2, 3):
            arrive(rx.at[g * 3 + k - 1], ("bx", g, k))
            total = total + rx[g * 3 + k - 1].astype(F32)
        return total

    for g in range(3):
        szl[g] = total_x(g).astype(BF)
        send(szl.at[g], rzl.at[g], ("bz", g), at("zl", ORDER[g])[0])

    piece = w1[pl.ds(pl.multiple_of(x * 32, 32), 32), :]
    for k in (1, 2, 3):
        arrive(w2r.at[k - 1], ("w2", k))
        piece = piece + w2r[k - 1].astype(F32)
    w2[...] = piece.reshape(4, 8, 256)
    for k in (2, 1, 3):
        d, there = at("y", k)
        send(w2.at[there], w3r.at[k - 1], ("w3", k), d)

    total = total_y(3)
    for g in range(3):
        arrive(rz.at[g], ("oz", g))
        total = total + rz[g].astype(F32)
    out_o[...] = total.astype(BF)

    small = w2[y]
    for k in (1, 2, 3):
        arrive(w3r.at[k - 1], ("w3", k))
        small = small + w3r[k - 1]
    w4[zl] = small
    for k in (2, 1, 3):
        send(w4.at[zl], w4.at[zl], ("w4", k), at("zl", k)[0])

    grad = total_x(3)
    for g in range(3):
        arrive(rzl.at[g], ("bz", g))
        grad = grad + rzl[g].astype(F32)
    high = grad.astype(BF)
    low = (grad - high.astype(F32)).astype(BF)
    nt = (((1,), (1,)), ((), ()))
    ig_o[...] = (
        lax.dot_general(high, weight[...], nt, preferred_element_type=F32)
        + lax.dot_general(low, weight[...], nt, preferred_element_type=F32)
    ).astype(BF)

    for k in (1, 2, 3):
        arrive(w4.at[r4(zl + 4 - k)], ("w4", k))
    w5[zh] = ((w4[0] + w4[1]) + w4[2]) + w4[3]
    for k in (2, 1, 3):
        send(w5.at[zh], w5.at[zh], ("w5", k), at("zh", k)[0])
    for k in (1, 2, 3):
        arrive(w5.at[r4(zh + 4 - k)], ("w5", k))
    scale = 1.0 / math.sqrt(65536)

    def rows_of(c_, x_, y_):
        return pl.multiple_of(c_ * 128 + x_ * 32 + y_ * 8, 8)

    mine = wg_o.at[pl.ds(rows_of(c, x, y), 8)]
    mine[...] = (((w5[0] + w5[1]) + w5[2]) + w5[3]) * scale
    for k in (2, 1, 3):
        send(mine, mine, ("w6", k), at("y", k)[0])
    for k in (1, 2, 3):
        arrive(wg_o.at[pl.ds(rows_of(c, x, r4(y + 4 - k)), 8)], ("w6", k))
    mine = wg_o.at[pl.ds(rows_of(c, x, 0), 32)]
    for k in (2, 1, 3):
        send(mine, mine, ("w7", k), at("x", k)[0])
    for k in (1, 2, 3):
        arrive(wg_o.at[pl.ds(rows_of(c, r4(x + 4 - k), 0), 32)], ("w7", k))
    mine = wg_o.at[pl.ds(rows_of(c, 0, 0), 128)]
    send(mine, mine, ("w8",), dev(c_=sib))
    arrive(wg_o.at[pl.ds(rows_of(sib, 0, 0), 128)], ("w8",))

    for copy in sends:
        copy.wait_send()


def body(features, weight, cotangent, block_index, block_count, block_values):
    vmem = pl.BlockSpec(memory_space=pltpu.VMEM)
    smem = pl.BlockSpec(memory_space=pltpu.SMEM)
    index = block_index.reshape(1, 32)
    blocks = functools.partial(lambda dtype, n: pltpu.VMEM((n, 128, 256), dtype))
    return pl.pallas_call(
        kernel,
        out_shape=(
            jax.ShapeDtypeStruct((128, 256), BF),
            jax.ShapeDtypeStruct((128, 256), BF),
            jax.ShapeDtypeStruct((256, 256), F32),
        ),
        in_specs=[vmem, vmem, vmem, vmem, smem, smem, vmem],
        out_specs=(vmem, vmem, vmem),
        scratch_shapes=[
            blocks(BF, 16), blocks(BF, 32), blocks(BF, 16), blocks(F32, 33),
            blocks(BF, 32), blocks(BF, 16),
            pltpu.VMEM((8, 128), jnp.int32), pltpu.SMEM((8, 128), jnp.int32),
            blocks(BF, 16), blocks(BF, 12), blocks(F32, 4), blocks(BF, 12),
            blocks(BF, 3), blocks(BF, 3), blocks(BF, 12), blocks(BF, 3), blocks(BF, 3),
            pltpu.VMEM((256, 256), F32), pltpu.VMEM((128, 256), BF), pltpu.VMEM((128, 256), BF),
            pltpu.VMEM((128, 256), F32), pltpu.VMEM((3, 32, 256), BF), pltpu.VMEM((3, 32, 256), BF),
            pltpu.VMEM((4, 8, 256), F32), pltpu.VMEM((3, 8, 256), F32),
            pltpu.VMEM((4, 8, 256), F32), pltpu.VMEM((4, 8, 256), F32),
            pltpu.SemaphoreType.DMA((COPIES,)), pltpu.SemaphoreType.DMA((COPIES,)),
            pltpu.SemaphoreType.DMA,
        ],
        compiler_params=pltpu.CompilerParams(
            collective_id=0, has_side_effects=True, vmem_limit_bytes=48 << 20
        ),
        name="graph_step",
    )(features, weight, cotangent, index, index, block_count, block_values[0, 0])


def solution(mesh):
    in_specs = (
        P(("col", "row"), None),
        P(),
        P(("row", "col"), None),
        P("row", "col", None),
        P("row", "col"),
        P("row", "col", None, None, None),
    )
    out_specs = (P(("row", "col"), None), P(("col", "row"), None), P())
    return jax.shard_map(body, mesh=mesh, in_specs=in_specs, out_specs=out_specs, check_vma=False)
```

time: 882 us -> 107 us (0.12)
  waiting for transfers between devices: 811 us -> 0 us
  Pallas kernels: 0 us -> 98.6 us
  matrix products: 24.6 us -> 0 us
  local copies, waits for them, and re-layouts: 24.8 us -> 6.42 us
  between operations: 14.5 us -> 1.3 us
    psum x1 -> x0, waiting for transfers between devices: 443 us -> none  [body(): total = lax.psum(term, ('row', 'col'))]
    reduce_scatter x2 -> x0, waiting for transfers between devices: 195 us -> none  [the longest x1 121 us: body(): lax.psum_scatter(partial_out.reshape(block_rows * size, width).astype(jnp...]
    all_gather x2 -> x0, waiting for transfers between devices: 172 us -> none  [the longest x1 86.3 us: body(): projected = lax.all_gather(own_projected, 'row', axis=0, tiled=True)]
    pallas_call x0 -> x1, Pallas kernels: none -> 98.6 us  [body(): pl.pallas_call(kernel, out_shape=(jax.ShapeDtypeStruct((128, 256), BF), j...]
    dot_general x7 -> x0, matrix products: 24.6 us -> none  [the longest x1 7.68 us: forward_advance(): jnp.einsum('rg,gid->rid', selector.astype(jnp.float32), product, precisio...]
    dot_general x2 -> x0, local copies, waits for them, and re-layouts: 11 us -> none  [the longest x1 5.5 us: backward_advance(): jnp.einsum('gij,gid->gjd', values, picked, preferred_element_type=jnp.flo...]
  transfers between devices with their start and end apart: 5 -> 0, of which waited for: 5 -> 0; matrix products, arithmetic and copies ran while one was open for 4% -> 0% of each run, Pallas kernels for 0% -> 0%
where the time goes in v1:
time: 107 us; the launch traced here: 106 us
  Pallas kernels  98.6 us (92%)
  local copies, waits for them, and re-layouts  6.42 us (6%)
  between operations  1.3 us (1%)
    pallas_call x1, Pallas kernels, body(): pl.pallas_call(kernel, out_shape=(jax.ShapeDtypeStruct((128, 256), BF), j...  98.6 us
    unnamed x13, local copies, waits for them, and re-layouts  6.42 us

profile of v1, /device:TPU:1, one launch (start us, length us, event | category | flops | bytes accessed | tf_op | source)
XLA Modules:
  0.0 106.4 jit_solution(17250230246209481982)
XLA Ops:
  1.3 0.0 copy-start.4
  1.3 0.6 copy-done.4
  1.9 0.0 copy-start
  1.9 1.2 %copy-done = bf16[1,1,32,128,128]{4,3,2,1,0:T(8,128)(2,1)S(1)} copy-done((bf16[1,1,32,128,128]{4,3,2,1,0:T(8,128)(2,1)S(1)}, bf16[1,1,32,128,128]{4,3,2,1,0:T(8,128)(2,1)}, u32[]{:S(2)}) %copy-start) | copy-done | bytes 1048600
  3.2 0.0 copy-start.1
  3.2 0.9 copy-done.1
  4.1 0.0 copy-start.2
  4.1 0.8 copy-done.2
  4.9 0.0 copy-start.3
  4.9 0.8 copy-done.3
  5.7 98.6 %graph_step.1 = (bf16[128,256]{1,0:T(8,128)(2,1)S(1)}, bf16[128,256]{1,0:T(8,128)(2,1)S(1)}, f32[256,256]{1,0:T(8,128)S(1)}) custom-call(bf16[128,256]{1,0:T(8,128)(2,1)S(1)} %copy-done.2, bf16[256,256]{1,0:T(8,128)(2,1)S(1)} %copy-done.1, bf16[128,256]{1,0:T(8,128)(2,1)S(1)} %copy-done.3, s32[1,32]{1,0:T(1,128)S(1)} %bitcast.3, s32[1,32]{1,0:T(1,128)S(1)} %bitcast.4, ...), custom_call_target="tpu_custom_call" | custom-call | tf_op jit(solution)/shard_map/graph_step/pallas_call | solution.py:329
  104.4 0.6 copy.13
  105.0 0.6 copy.14
  105.7 0.7 copy.15
Async XLA Ops:
  1.3 0.7 copy-start.4
  1.9 1.2 %copy-start = (bf16[1,1,32,128,128]{4,3,2,1,0:T(8,128)(2,1)S(1)}, bf16[1,1,32,128,128]{4,3,2,1,0:T(8,128)(2,1)}, u32[]{:S(2)}) copy-start(bf16[1,1,32,128,128]{4,3,2,1,0:T(8,128)(2,1)} %param.11) | copy-start | bytes 3145732
  3.2 0.9 copy-start.1
  4.1 0.8 copy-start.2
  4.9 0.8 copy-start.3

commit v2 on v1

v2 whole, which is shorter than its diff:
```python
import functools
import math

import jax
import jax.numpy as jnp
from jax import lax
from jax.experimental import pallas as pl
from jax.experimental.pallas import tpu as pltpu
from jax.sharding import PartitionSpec as P

MESH = pl.DeviceIdType.MESH
BF = jnp.bfloat16
F32 = jnp.float32
RING = 4
ORDER = (2, 1, 3, 0)


def ids():
    table = {}

    def of(*key):
        return table.setdefault(key, len(table))

    return of


COPIES = 119


def kernel(
    feat_h, weight_h, cot_h, vals_h, idx_h, cnt,
    out_o, ig_o, wg_o,
    weight, vals, vals_t, fa, fa_t, ca, proj, run, pout, pback, tbl_v, tbl_s,
    rc, sy, own_y, ry, sz, rz, relay, rx, szl, rzl,
    wacc, wb, w1r, w3, w4, w5,
    idxs, ss, rs, ls, ins,
):
    of = ids()
    row = lax.axis_index("row")
    col = lax.axis_index("col")
    x, zl = row // 4, lax.rem(row, 4)
    y, zh, c = col // 8, lax.rem(col // 2, 4), lax.rem(col, 2)
    sib = 1 - c

    def r4(v):
        return lax.rem(v, 4)

    def dev(x_=x, zl_=zl, y_=y, zh_=zh, c_=c):
        return (x_ * 4 + zl_, y_ * 8 + zh_ * 2 + c_)

    def at(axis, k):
        here = {"x": x, "zl": zl, "y": y, "zh": zh}[axis]
        there = r4(here + k)
        return dev(**{axis + "_": there}), there

    sends = []
    def send(src, dst, key, device):
        n = of(*key)
        copy = pltpu.make_async_remote_copy(
            src_ref=src, dst_ref=dst, send_sem=ss.at[n], recv_sem=rs.at[n],
            device_id=device, device_id_type=MESH,
        )
        copy.start()
        sends.append(copy)

    def arrive(dst, key):
        n = of(*key)
        pltpu.make_async_remote_copy(
            src_ref=dst, dst_ref=dst, send_sem=ss.at[n], recv_sem=rs.at[n],
            device_id=dev(c_=sib), device_id_type=MESH,
        ).wait_recv()

    loads = [
        pltpu.make_async_copy(src, dst, ins.at[n])
        for n, (src, dst) in enumerate(
            [
                (feat_h, fa.at[row]), (cot_h, ca.at[col]), (weight_h, weight),
                (vals_h, vals), (idx_h, idxs),
            ]
        )
    ]
    for load in loads:
        load.start()

    barrier = pltpu.get_barrier_semaphore()
    partners = [at(a, k)[0] for a in ("x", "zl", "y", "zh") for k in (1, 2, 3)]
    partners.append(dev(c_=sib))
    shifts = [(kx, ky) for kx in (1, 3, 2, 0) for ky in (1, 3, 2, 0) if kx or ky]
    plane = {
        (kx, ky): dev(x_=r4(x + kx), y_=r4(y + ky)) for kx, ky in shifts
    }
    partners += [plane[kx, ky] for kx, ky in shifts if kx and ky]
    for p in partners:
        pl.semaphore_signal(barrier, inc=1, device_id=p, device_id_type=MESH)

    loads[0].wait()
    loads[1].wait()
    pl.semaphore_wait(barrier, len(partners))

    def features_on(block, tag):
        for k in (1, 2, 3):
            d, _ = at("x", k)
            send(fa.at[block], fa.at[block], ("fx", k, tag), d)

    def cotangents_on(block, tag):
        for k in (1, 2, 3):
            d, _ = at("y", k)
            send(ca.at[block], ca.at[block], ("cy", k, tag), d)
        send(ca.at[block], ca.at[block], ("cs", 0, tag), dev(c_=sib))

    for k in (1, 3):
        send(ca.at[col], ca.at[col], ("cz", k), at("zh", k)[0])
    for k in (1, 3, 2):
        send(fa.at[row], fa.at[row], ("fz", k), at("zl", k)[0])
    cotangents_on(col, 0)
    features_on(row, 0)

    for load in loads[2:]:
        load.wait()
    lane = lax.broadcasted_iota(jnp.int32, (1, 128), 1)
    count = cnt[0, 0]
    none = jnp.full((1, 128), 32, jnp.int32)
    zero = jnp.zeros((1, 128), jnp.int32)

    def place(t, carry):
        srow, scol = carry
        i = idxs[0, t]
        here = lane == t
        return jnp.where(here, i // 16, srow), jnp.where(here, lax.rem(i, 16), scol)

    srow, scol = lax.fori_loop(0, 32, place, (zero, zero))

    def link(t, carry):
        pf, lf, pb, lb = carry
        i = idxs[0, t]
        ti, tj = i // 16, lax.rem(i, 16)
        later = lane > t
        pf = jnp.where(later & (srow == ti), t, pf)
        pb = jnp.where(later & (scol == tj), t, pb)
        live = jnp.full((1, 128), t, jnp.int32) < count
        lf = jnp.where(live & (lane == ti), t, lf)
        lb = jnp.where(live & (lane == tj), t, lb)
        return pf, lf, pb, lb

    pf, lf, pb, lb = lax.fori_loop(0, 32, link, (none, none, none, none))
    for n, line in enumerate((scol, pf, lf, srow, pb, lb)):
        tbl_v[n : n + 1, :] = line
    table = pltpu.make_async_copy(tbl_v, tbl_s, ls)
    table.start()
    run[32] = jnp.zeros_like(run[32])

    def turn(s, carry):
        vals_t[s] = vals[s].T
        return carry

    def project(block):
        proj[block] = jnp.dot(fa[block], weight[...], preferred_element_type=F32).astype(BF)
        fa_t[block] = fa[block].T

    lax.fori_loop(0, 32, turn, 0, unroll=4)

    def features_in(k):
        block = x * 4 + r4(zl + 4 - k)
        arrive(fa.at[block], ("fz", k))
        features_on(block, k)

    far = y * 8 + r4(zh + 2) * 2 + c
    halves = (pl.ds(0, 64), pl.ds(64, 64))
    for n, k in enumerate((1, 3)):
        block = y * 8 + r4(zh + 4 - k) * 2 + c
        arrive(ca.at[block], ("cz", k))
        half = ca.at[block, halves[n]]
        send(half, half, ("ch", n), at("zh", k)[0])
        cotangents_on(block, k)

    def across(tag):
        for k in (1, 3, 2):
            block = r4(y + 4 - k) * 8 + r4(zh + 4 - tag) * 2 + c
            arrive(ca.at[block], ("cy", k, tag))
            send(ca.at[block], ca.at[block], ("cs", k, tag), dev(c_=sib))

    across(0)
    for k in (1, 3, 2):
        features_in(k)
    for k in (0, 1, 3, 2):
        project(x * 4 + r4(zl + 4 - k))
    for n in (0, 1):
        arrive(ca.at[far, halves[n]], ("ch", n))
    cotangents_on(far, 2)
    across(1)
    across(3)
    for tag in (0, 1, 3, 2):
        for k in (1, 3, 2):
            block = r4(x + 4 - k) * 4 + r4(zl + 4 - tag)
            arrive(fa.at[block], ("fx", k, tag))
            project(block)
    table.wait()

    def chain(left, right, at_line, previous_line):
        def some(q, carry):
            products = [
                jnp.dot(left[q * 8 + u], right[tbl_s[at_line, q * 8 + u]], preferred_element_type=F32)
                for u in range(8)
            ]
            for u in range(8):
                run[q * 8 + u] = products[u] + run[tbl_s[previous_line, q * 8 + u]]
            return carry

        lax.fori_loop(0, 4, some, 0)

    chain(vals, proj, 0, 1)

    def forward_out(o, carry):
        r = lax.rem(o, 4) * 8 + lax.rem(o // 4, 4) * 2 + o // 16
        pout[o] = run[tbl_s[2, r]].astype(BF)
        return carry

    lax.fori_loop(0, 32, forward_out, 0)

    def group(g):
        return r4(zh + ORDER[g])

    for g in range(4):
        part = pl.ds(sib * 16 + group(g) * 4, 4)
        send(pout.at[part], rc.at[pl.ds(g * 4, 4)], ("oc", g), dev(c_=sib))

    def out_y(g):
        arrive(rc.at[pl.ds(g * 4, 4)], ("oc", g))
        for k in (2, 1, 3):
            d, there = at("y", k)
            own = pout[c * 16 + group(g) * 4 + there].astype(F32)
            sy[g * 3 + k - 1] = (own + rc[g * 4 + there].astype(F32)).astype(BF)
            send(sy.at[g * 3 + k - 1], ry.at[g * 3 + k - 1], ("oy", g, k), d)
        own_y[g] = pout[c * 16 + group(g) * 4 + y].astype(F32) + rc[g * 4 + y].astype(F32)

    across(2)
    out_y(0)
    out_y(1)

    def total_y(g):
        total = own_y[g]
        for k in (1, 2, 3):
            arrive(ry.at[g * 3 + k - 1], ("oy", g, k))
            total = total + ry[g * 3 + k - 1].astype(F32)
        return total

    def out_z(g):
        sz[g] = total_y(g).astype(BF)
        if g == 0:
            for n, k in enumerate((1, 3)):
                send(sz.at[0, halves[n]], relay.at[n], ("or", n), at("zh", k)[0])
            return
        n = g - 1
        arrive(relay.at[n], ("or", n))
        sz[g, halves[n], :] = (sz[g, halves[n], :].astype(F32) + relay[n].astype(F32)).astype(BF)
        send(sz.at[g], rz.at[n], ("oz", n), at("zh", ORDER[g])[0])

    def out_end():
        total = total_y(3)
        for n in range(2):
            arrive(rz.at[n], ("oz", n))
            total = total + rz[n].astype(F32)
        out_o[...] = total.astype(BF)

    for tag in (0, 1, 3, 2):
        for k in (0, 1, 3, 2):
            block = r4(y + 4 - k) * 8 + r4(zh + 4 - tag) * 2 + sib
            arrive(ca.at[block], ("cs", k, tag))

    chain(vals_t, ca, 3, 4)

    def backward_out(j, carry):
        pback[j] = run[tbl_s[5, j]].astype(BF)
        return carry

    lax.fori_loop(0, 16, backward_out, 0)

    term = jnp.zeros((256, 256), F32)
    for j in range(16):
        term += jnp.dot(fa_t[j], pback[j], preferred_element_type=F32)
    wacc[...] = term
    wb[...] = term.astype(BF)

    def piece(x_, y_):
        return pl.ds(pl.multiple_of(x_ * 64 + y_ * 16, 16), 16)

    for kx, ky in shifts:
        part = wb.at[piece(r4(x + kx), r4(y + ky))]
        send(part, w1r.at[kx * 4 + ky], ("w1", kx, ky), plane[kx, ky])

    def term_zl():
        small = wacc[piece(x, y), :]
        for kx, ky in shifts:
            arrive(w1r.at[kx * 4 + ky], ("w1", kx, ky))
            small = small + w1r[kx * 4 + ky].astype(F32)
        w3[zl] = small.astype(BF)
        for k in (2, 1, 3):
            send(w3.at[zl], w3.at[zl], ("w3", k), at("zl", k)[0])

    def four(ref):
        low = ref[0].astype(F32) + ref[1].astype(F32)
        return low + ref[2].astype(F32) + ref[3].astype(F32)

    def term_zh():
        for k in (1, 2, 3):
            arrive(w3.at[r4(zl + 4 - k)], ("w3", k))
        w4[zh] = four(w3).astype(BF)
        for k in (2, 1, 3):
            send(w4.at[zh], w4.at[zh], ("w4", k), at("zh", k)[0])

    def term_core():
        for k in (1, 2, 3):
            arrive(w4.at[r4(zh + 4 - k)], ("w4", k))
        w5[0] = four(w4)
        send(w5.at[0], w5.at[1], ("w5",), dev(c_=sib))

    def back_xy():
        arrive(w5.at[1], ("w5",))
        mine = wg_o.at[piece(x, y)]
        mine[...] = (w5[0] + w5[1]) * (1.0 / math.sqrt(65536))
        for kx, ky in shifts:
            send(mine, mine, ("w6", kx, ky), plane[kx, ky])

    def back_end():
        for kx, ky in shifts:
            arrive(wg_o.at[piece(r4(x + 4 - kx), r4(y + 4 - ky))], ("w6", kx, ky))

    def grad_x(g):
        zt = r4(zl + ORDER[g])
        for k in (2, 1, 3):
            d, there = at("x", k)
            send(pback.at[there * 4 + zt], rx.at[g * 3 + k - 1], ("bx", g, k), d)

    def total_x(g):
        total = pback[x * 4 + r4(zl + ORDER[g])].astype(F32)
        for k in (1, 2, 3):
            arrive(rx.at[g * 3 + k - 1], ("bx", g, k))
            total = total + rx[g * 3 + k - 1].astype(F32)
        return total

    def grad_z(g):
        szl[g] = total_x(g).astype(BF)
        send(szl.at[g], rzl.at[g], ("bz", g), at("zl", ORDER[g])[0])

    def grad_end():
        grad = total_x(3)
        for g in range(3):
            arrive(rzl.at[g], ("bz", g))
            grad = grad + rzl[g].astype(F32)
        high = grad.astype(BF)
        low = (grad - high.astype(F32)).astype(BF)
        nt = (((1,), (1,)), ((), ()))
        ig_o[...] = (
            lax.dot_general(high, weight[...], nt, preferred_element_type=F32)
            + lax.dot_general(low, weight[...], nt, preferred_element_type=F32)
        ).astype(BF)

    out_y(2)
    out_y(3)
    for g in range(4):
        grad_x(g)
    out_z(0)
    term_zl()
    term_zh()
    out_z(1)
    out_z(2)
    grad_z(0)
    grad_z(1)
    grad_z(2)
    term_core()
    back_xy()
    out_end()
    grad_end()
    back_end()

    for copy in sends:
        copy.wait_send()


def body(features, weight, cotangent, block_index, block_count, block_values):
    hbm = pl.BlockSpec(memory_space=pltpu.HBM)
    index = block_index.reshape(1, 32)
    operands = [
        pltpu.with_memory_space_constraint(a, pltpu.HBM)
        for a in (features, weight, cotangent, block_values.reshape(32, 128, 128), index)
    ]
    blocks = functools.partial(lambda dtype, n: pltpu.VMEM((n, 128, 256), dtype))
    shapes = (
        jax.ShapeDtypeStruct((128, 256), BF),
        jax.ShapeDtypeStruct((128, 256), BF),
        jax.ShapeDtypeStruct((256, 256), F32),
    )
    vmem = pl.BlockSpec(memory_space=pltpu.VMEM)
    return pl.pallas_call(
        kernel,
        out_shape=shapes,
        in_specs=[hbm] * 5 + [pl.BlockSpec(memory_space=pltpu.SMEM)],
        out_specs=(vmem, vmem, vmem),
        scratch_shapes=[
            pltpu.VMEM((256, 256), BF), pltpu.VMEM((32, 128, 128), BF), pltpu.VMEM((32, 128, 128), BF),
            blocks(BF, 16), pltpu.VMEM((16, 256, 128), BF), blocks(BF, 32), blocks(BF, 16), blocks(F32, 33),
            blocks(BF, 32), blocks(BF, 16),
            pltpu.VMEM((8, 128), jnp.int32), pltpu.SMEM((8, 128), jnp.int32),
            blocks(BF, 16), blocks(BF, 12), blocks(F32, 4), blocks(BF, 12),
            blocks(BF, 3), blocks(BF, 2), pltpu.VMEM((2, 64, 256), BF), blocks(BF, 12), blocks(BF, 3), blocks(BF, 3),
            pltpu.VMEM((256, 256), F32), pltpu.VMEM((256, 256), BF), pltpu.VMEM((16, 16, 256), BF),
            pltpu.VMEM((4, 16, 256), BF), pltpu.VMEM((4, 16, 256), BF), pltpu.VMEM((2, 16, 256), F32),
            pltpu.SMEM((1, 32), jnp.int32),
            pltpu.SemaphoreType.DMA((COPIES,)), pltpu.SemaphoreType.DMA((COPIES,)),
            pltpu.SemaphoreType.DMA, pltpu.SemaphoreType.DMA((5,)),
        ],
        compiler_params=pltpu.CompilerParams(
            collective_id=0, has_side_effects=True, vmem_limit_bytes=48 << 20
        ),
        name="graph_step",
    )(*operands, block_count)


def solution(mesh):
    in_specs = (
        P(("col", "row"), None),
        P(),
        P(("row", "col"), None),
        P("row", "col", None),
        P("row", "col"),
        P("row", "col", None, None, None),
    )
    out_specs = (P(("row", "col"), None), P(("col", "row"), None), P())
    return jax.shard_map(body, mesh=mesh, in_specs=in_specs, out_specs=out_specs, check_vma=False)
```

time: 107 us -> 75 us (0.70)
  Pallas kernels: 98.6 us -> 71.6 us
  local copies, waits for them, and re-layouts: 6.42 us -> 1.96 us
    pallas_call x1, Pallas kernels: 98.6 us -> 71.6 us  [body(): pl.pallas_call(kernel, out_shape=shapes, in_specs=[hbm] * 5 + [pl.BlockSp...]
    unnamed x13 -> x3, local copies, waits for them, and re-layouts: 6.42 us -> 1.96 us
where the time goes in v2:
time: 75 us; the launch traced here: 74.8 us
  Pallas kernels  71.6 us (95%)
  local copies, waits for them, and re-layouts  1.96 us (3%)
  between operations  1.29 us (2%)
    pallas_call x1, Pallas kernels, body(): pl.pallas_call(kernel, out_shape=shapes, in_specs=[hbm] * 5 + [pl.BlockSp...  71.6 us
    unnamed x3, local copies, waits for them, and re-layouts  1.96 us

profile of v2, /device:TPU:1, one launch (start us, length us, event | category | flops | bytes accessed | tf_op | source)
XLA Modules:
  0.0 74.8 jit_solution(17103872985454764568)
XLA Ops:
  1.3 71.6 %graph_step.1 = (bf16[128,256]{1,0:T(8,128)(2,1)S(1)}, bf16[128,256]{1,0:T(8,128)(2,1)S(1)}, f32[256,256]{1,0:T(8,128)S(1)}) custom-call(bf16[128,256]{1,0:T(8,128)(2,1)} %feat_h.1, bf16[256,256]{1,0:T(8,128)(2,1)} %weight_h.1, bf16[128,256]{1,0:T(8,128)(2,1)} %cot_h.1, bf16[32,128,128]{2,1,0:T(8,128)(2,1)} %bitcast.2, s32[1,32]{1,0:T(1,128)} %bitcast.3, ...), custom_call_target="tpu_custom_call" | custom-call | tf_op jit(solution)/shard_map/graph_step/pallas_call | solution.py:394
  72.9 0.6 copy.13
  73.5 0.6 copy.14
  74.1 0.7 copy.15

commit v3 on v2

--- a/solution.py
+++ b/solution.py
@@ -19,12 +19,14 @@
     table = {}
 
     def of(*key):
-        return table.setdefault(key, len(table))
+        n = table.setdefault(key, len(table))
+        assert n < KEYS
+        return n
 
     return of
 
 
-COPIES = 119
+KEYS = 37
 
 
 def kernel(
@@ -32,8 +34,8 @@
     out_o, ig_o, wg_o,
     weight, vals, vals_t, fa, fa_t, ca, proj, run, pout, pback, tbl_v, tbl_s,
     rc, sy, own_y, ry, sz, rz, relay, rx, szl, rzl,
-    wacc, wb, w1r, w3, w4, w5,
-    idxs, ss, rs, ls, ins,
+    wacc, wb, w0r, wh, w1s, w1r, w3, w6, w8r,
+    idxs, ss, rs, ls, ins, near,
 ):
     of = ids()
     row = lax.axis_index("row")
@@ -53,22 +55,23 @@
         there = r4(here + k)
         return dev(**{axis + "_": there}), there
 
-    sends = []
-    def send(src, dst, key, device):
-        n = of(*key)
-        copy = pltpu.make_async_remote_copy(
-            src_ref=src, dst_ref=dst, send_sem=ss.at[n], recv_sem=rs.at[n],
+    def send(src, dst, key, device, group=0):
+        pltpu.make_async_remote_copy(
+            src_ref=src, dst_ref=dst, send_sem=ss.at[group], recv_sem=rs.at[of(*key)],
             device_id=device, device_id_type=MESH,
-        )
-        copy.start()
-        sends.append(copy)
-
-    def arrive(dst, key):
-        n = of(*key)
+        ).start()
+
+    def arrive(ref, key):
         pltpu.make_async_remote_copy(
-            src_ref=dst, dst_ref=dst, send_sem=ss.at[n], recv_sem=rs.at[n],
+            src_ref=ref, dst_ref=ref, send_sem=ss.at[0], recv_sem=rs.at[of(*key)],
             device_id=dev(c_=sib), device_id_type=MESH,
         ).wait_recv()
+
+    def sent(ref, group):
+        pltpu.make_async_remote_copy(
+            src_ref=ref, dst_ref=ref, send_sem=ss.at[group], recv_sem=rs.at[0],
+            device_id=dev(c_=sib), device_id_type=MESH,
+        ).wait_send()
 
     loads = [
         pltpu.make_async_copy(src, dst, ins.at[n])
@@ -83,13 +86,9 @@
         load.start()
 
     barrier = pltpu.get_barrier_semaphore()
-    partners = [at(a, k)[0] for a in ("x", "zl", "y", "zh") for k in (1, 2, 3)]
-    partners.append(dev(c_=sib))
-    shifts = [(kx, ky) for kx in (1, 3, 2, 0) for ky in (1, 3, 2, 0) if kx or ky]
-    plane = {
-        (kx, ky): dev(x_=r4(x + kx), y_=r4(y + ky)) for kx, ky in shifts
-    }
-    partners += [plane[kx, ky] for kx, ky in shifts if kx and ky]
+    x_peers, zl_peers, y_peers = ([at(a, k)[0] for k in (1, 2, 3)] for a in ("x", "zl", "y"))
+    zh_peers = [at("zh", k)[0] for k in (1, 3)]
+    partners = [*x_peers, *zl_peers, *y_peers, *zh_peers, dev(c_=sib)]
     for p in partners:
         pl.semaphore_signal(barrier, inc=1, device_id=p, device_id_type=MESH)
 
@@ -97,16 +96,24 @@
     loads[1].wait()
     pl.semaphore_wait(barrier, len(partners))
 
+    def tell(n, devices):
+        for p in devices:
+            pl.semaphore_signal(near.at[n], inc=1, device_id=p, device_id_type=MESH)
+
+    tell(0, zh_peers)
+    tell(2, x_peers)
+    shifts = [(a, b) for a in (1, 3, 2, 0) for b in (1, 3, 2, 0) if a or b]
+
     def features_on(block, tag):
         for k in (1, 2, 3):
             d, _ = at("x", k)
-            send(fa.at[block], fa.at[block], ("fx", k, tag), d)
+            send(fa.at[block], fa.at[block], ("fx", tag), d)
 
     def cotangents_on(block, tag):
         for k in (1, 2, 3):
             d, _ = at("y", k)
-            send(ca.at[block], ca.at[block], ("cy", k, tag), d)
-        send(ca.at[block], ca.at[block], ("cs", 0, tag), dev(c_=sib))
+            send(ca.at[block], ca.at[block], ("cy", tag), d)
+        send(ca.at[block], ca.at[block], ("cs",), dev(c_=sib))
 
     for k in (1, 3):
         send(ca.at[col], ca.at[col], ("cz", k), at("zh", k)[0])
@@ -170,30 +177,30 @@
         block = y * 8 + r4(zh + 4 - k) * 2 + c
         arrive(ca.at[block], ("cz", k))
         half = ca.at[block, halves[n]]
-        send(half, half, ("ch", n), at("zh", k)[0])
+        send(half, half, ("ch",), at("zh", k)[0])
         cotangents_on(block, k)
 
     def across(tag):
+        arrive(ca.at[pl.ds(0, 3)], ("cy", tag))
         for k in (1, 3, 2):
             block = r4(y + 4 - k) * 8 + r4(zh + 4 - tag) * 2 + c
-            arrive(ca.at[block], ("cy", k, tag))
-            send(ca.at[block], ca.at[block], ("cs", k, tag), dev(c_=sib))
-
+            send(ca.at[block], ca.at[block], ("cs",), dev(c_=sib))
+
+    pl.semaphore_wait(near.at[0], 2)
+    tell(1, zl_peers)
     across(0)
     for k in (1, 3, 2):
         features_in(k)
     for k in (0, 1, 3, 2):
         project(x * 4 + r4(zl + 4 - k))
-    for n in (0, 1):
-        arrive(ca.at[far, halves[n]], ("ch", n))
+    arrive(ca.at[far], ("ch",))
     cotangents_on(far, 2)
     across(1)
     across(3)
     for tag in (0, 1, 3, 2):
+        arrive(fa.at[pl.ds(0, 3)], ("fx", tag))
         for k in (1, 3, 2):
-            block = r4(x + 4 - k) * 4 + r4(zl + 4 - tag)
-            arrive(fa.at[block], ("fx", k, tag))
-            project(block)
+            project(r4(x + 4 - k) * 4 + r4(zl + 4 - tag))
     table.wait()
 
     def chain(left, right, at_line, previous_line):
@@ -222,7 +229,7 @@
 
     for g in range(4):
         part = pl.ds(sib * 16 + group(g) * 4, 4)
-        send(pout.at[part], rc.at[pl.ds(g * 4, 4)], ("oc", g), dev(c_=sib))
+        send(pout.at[part], rc.at[pl.ds(g * 4, 4)], ("oc", g), dev(c_=sib), 1)
 
     def out_y(g):
         arrive(rc.at[pl.ds(g * 4, 4)], ("oc", g))
@@ -230,7 +237,7 @@
             d, there = at("y", k)
             own = pout[c * 16 + group(g) * 4 + there].astype(F32)
             sy[g * 3 + k - 1] = (own + rc[g * 4 + there].astype(F32)).astype(BF)
-            send(sy.at[g * 3 + k - 1], ry.at[g * 3 + k - 1], ("oy", g, k), d)
+            send(sy.at[g * 3 + k - 1], ry.at[g * 3 + k - 1], ("oy", g), d, 1)
         own_y[g] = pout[c * 16 + group(g) * 4 + y].astype(F32) + rc[g * 4 + y].astype(F32)
 
     across(2)
@@ -239,8 +246,8 @@
 
     def total_y(g):
         total = own_y[g]
+        arrive(ry.at[pl.ds(g * 3, 3)], ("oy", g))
         for k in (1, 2, 3):
-            arrive(ry.at[g * 3 + k - 1], ("oy", g, k))
             total = total + ry[g * 3 + k - 1].astype(F32)
         return total
 
@@ -248,24 +255,21 @@
         sz[g] = total_y(g).astype(BF)
         if g == 0:
             for n, k in enumerate((1, 3)):
-                send(sz.at[0, halves[n]], relay.at[n], ("or", n), at("zh", k)[0])
+                send(sz.at[0, halves[n]], relay.at[n], ("or", n), at("zh", k)[0], 1)
             return
         n = g - 1
         arrive(relay.at[n], ("or", n))
         sz[g, halves[n], :] = (sz[g, halves[n], :].astype(F32) + relay[n].astype(F32)).astype(BF)
-        send(sz.at[g], rz.at[n], ("oz", n), at("zh", ORDER[g])[0])
+        send(sz.at[g], rz.at[n], ("oz",), at("zh", ORDER[g])[0], 1)
 
     def out_end():
         total = total_y(3)
+        arrive(rz, ("oz",))
         for n in range(2):
-            arrive(rz.at[n], ("oz", n))
             total = total + rz[n].astype(F32)
         out_o[...] = total.astype(BF)
 
-    for tag in (0, 1, 3, 2):
-        for k in (0, 1, 3, 2):
-            block = r4(y + 4 - k) * 8 + r4(zh + 4 - tag) * 2 + sib
-            arrive(ca.at[block], ("cs", k, tag))
+    arrive(ca.at[pl.ds(0, 16)], ("cs",))
 
     chain(vals_t, ca, 3, 4)
 
@@ -280,72 +284,77 @@
         term += jnp.dot(fa_t[j], pback[j], preferred_element_type=F32)
     wacc[...] = term
     wb[...] = term.astype(BF)
-
-    def piece(x_, y_):
-        return pl.ds(pl.multiple_of(x_ * 64 + y_ * 16, 16), 16)
-
-    for kx, ky in shifts:
-        part = wb.at[piece(r4(x + kx), r4(y + ky))]
-        send(part, w1r.at[kx * 4 + ky], ("w1", kx, ky), plane[kx, ky])
-
-    def term_zl():
-        small = wacc[piece(x, y), :]
+    send(wb.at[pl.ds(pl.multiple_of(sib * 128, 128), 128)], w0r, ("w0",), dev(c_=sib), 2)
+
+    def term_xy():
+        arrive(w0r, ("w0",))
+        half = wacc[pl.ds(pl.multiple_of(c * 128, 128), 128), :] + w0r[...].astype(F32)
+        for p in range(16):
+            piece = half[p // 2 * 16 : p // 2 * 16 + 16, p % 2 * 128 : p % 2 * 128 + 128]
+            wh[p] = piece
+            w1s[p] = piece.astype(BF)
+        pl.semaphore_wait(near.at[2], 3)
         for kx, ky in shifts:
-            arrive(w1r.at[kx * 4 + ky], ("w1", kx, ky))
-            small = small + w1r[kx * 4 + ky].astype(F32)
-        w3[zl] = small.astype(BF)
-        for k in (2, 1, 3):
-            send(w3.at[zl], w3.at[zl], ("w3", k), at("zl", k)[0])
-
-    def four(ref):
-        low = ref[0].astype(F32) + ref[1].astype(F32)
-        return low + ref[2].astype(F32) + ref[3].astype(F32)
-
-    def term_zh():
-        for k in (1, 2, 3):
-            arrive(w3.at[r4(zl + 4 - k)], ("w3", k))
-        w4[zh] = four(w3).astype(BF)
-        for k in (2, 1, 3):
-            send(w4.at[zh], w4.at[zh], ("w4", k), at("zh", k)[0])
-
-    def term_core():
-        for k in (1, 2, 3):
-            arrive(w4.at[r4(zh + 4 - k)], ("w4", k))
-        w5[0] = four(w4)
-        send(w5.at[0], w5.at[1], ("w5",), dev(c_=sib))
+            there_x, there_y = r4(x + kx), r4(y + ky)
+            send(
+                w1s.at[there_x * 4 + there_y], w1r.at[kx * 4 + ky - 1], ("w1",),
+                dev(x_=there_x, y_=there_y), 3,
+            )
+
+    def term_z():
+        arrive(w1r, ("w1",))
+        small = wh[x * 4 + y]
+        for n in range(15):
+            small = small + w1r[n].astype(F32)
+        mine = w3.at[zl * 4 + zh]
+        mine[...] = small.astype(BF)
+        pl.semaphore_wait(near.at[1], 3)
+        for kl, kh in shifts:
+            send(mine, mine, ("w3",), dev(zl_=r4(zl + kl), zh_=r4(zh + kh)), 4)
 
     def back_xy():
-        arrive(w5.at[1], ("w5",))
-        mine = wg_o.at[piece(x, y)]
-        mine[...] = (w5[0] + w5[1]) * (1.0 / math.sqrt(65536))
+        arrive(w3.at[pl.ds(0, 15)], ("w3",))
+        total = w3[0].astype(F32)
+        for n in range(1, 16):
+            total = total + w3[n].astype(F32)
+        mine = w6.at[x * 4 + y]
+        mine[...] = (total * (1.0 / math.sqrt(65536))).astype(BF)
         for kx, ky in shifts:
-            send(mine, mine, ("w6", kx, ky), plane[kx, ky])
+            send(mine, mine, ("w6",), dev(x_=r4(x + kx), y_=r4(y + ky)), 5)
+
+    def back_core():
+        arrive(w6.at[pl.ds(0, 15)], ("w6",))
+        send(w6, w8r, ("w8",), dev(c_=sib), 2)
 
     def back_end():
-        for kx, ky in shifts:
-            arrive(wg_o.at[piece(r4(x + 4 - kx), r4(y + 4 - ky))], ("w6", kx, ky))
+        for here, ref in ((c, w6), (sib, w8r)):
+            if ref is w8r:
+                arrive(w8r, ("w8",))
+            for p in range(16):
+                at_row = pl.multiple_of(here * 128 + p // 2 * 16, 16)
+                wg_o[pl.ds(at_row, 16), p % 2 * 128 : p % 2 * 128 + 128] = ref[p].astype(F32)
 
     def grad_x(g):
         zt = r4(zl + ORDER[g])
         for k in (2, 1, 3):
             d, there = at("x", k)
-            send(pback.at[there * 4 + zt], rx.at[g * 3 + k - 1], ("bx", g, k), d)
+            send(pback.at[there * 4 + zt], rx.at[g * 3 + k - 1], ("bx", g), d, 1)
 
     def total_x(g):
         total = pback[x * 4 + r4(zl + ORDER[g])].astype(F32)
+        arrive(rx.at[pl.ds(g * 3, 3)], ("bx", g))
         for k in (1, 2, 3):
-            arrive(rx.at[g * 3 + k - 1], ("bx", g, k))
             total = total + rx[g * 3 + k - 1].astype(F32)
         return total
 
     def grad_z(g):
         szl[g] = total_x(g).astype(BF)
-        send(szl.at[g], rzl.at[g], ("bz", g), at("zl", ORDER[g])[0])
+        send(szl.at[g], rzl.at[g], ("bz",), at("zl", ORDER[g])[0], 1)
 
     def grad_end():
         grad = total_x(3)
+        arrive(rzl, ("bz",))
         for g in range(3):
-            arrive(rzl.at[g], ("bz", g))
             grad = grad + rzl[g].astype(F32)
         high = grad.astype(BF)
         low = (grad - high.astype(F32)).astype(BF)
@@ -355,26 +364,26 @@
             + lax.dot_general(low, weight[...], nt, preferred_element_type=F32)
         ).astype(BF)
 
+    term_xy()
     out_y(2)
     out_y(3)
     for g in range(4):
         grad_x(g)
     out_z(0)
-    term_zl()
-    term_zh()
+    term_z()
     out_z(1)
     out_z(2)
     grad_z(0)
     grad_z(1)
     grad_z(2)
-    term_core()
     back_xy()
     out_end()
+    back_core()
     grad_end()
     back_end()
 
-    for copy in sends:
-        copy.wait_send()
+    for group, ref in enumerate((run.at[pl.ds(0, 23)], run.at[pl.ds(0, 23)], fa.at[pl.ds(0, 2)], w1r, w1r, w1r)):
+        sent(ref, group)
 
 
 def body(features, weight, cotangent, block_index, block_count, block_values):
@@ -403,11 +412,11 @@
             pltpu.VMEM((8, 128), jnp.int32), pltpu.SMEM((8, 128), jnp.int32),
             blocks(BF, 16), blocks(BF, 12), blocks(F32, 4), blocks(BF, 12),
             blocks(BF, 3), blocks(BF, 2), pltpu.VMEM((2, 64, 256), BF), blocks(BF, 12), blocks(BF, 3), blocks(BF, 3),
-            pltpu.VMEM((256, 256), F32), pltpu.VMEM((256, 256), BF), pltpu.VMEM((16, 16, 256), BF),
-            pltpu.VMEM((4, 16, 256), BF), pltpu.VMEM((4, 16, 256), BF), pltpu.VMEM((2, 16, 256), F32),
+            pltpu.VMEM((256, 256), F32), pltpu.VMEM((256, 256), BF), pltpu.VMEM((128, 256), BF),
+            pltpu.VMEM((16, 16, 128), F32), *(pltpu.VMEM((n, 16, 128), BF) for n in (16, 15, 16, 16, 16)),
             pltpu.SMEM((1, 32), jnp.int32),
-            pltpu.SemaphoreType.DMA((COPIES,)), pltpu.SemaphoreType.DMA((COPIES,)),
-            pltpu.SemaphoreType.DMA, pltpu.SemaphoreType.DMA((5,)),
+            pltpu.SemaphoreType.DMA((6,)), pltpu.SemaphoreType.DMA((KEYS,)),
+            pltpu.SemaphoreType.DMA, pltpu.SemaphoreType.DMA((5,)), pltpu.SemaphoreType.REGULAR((3,)),
         ],
         compiler_params=pltpu.CompilerParams(
             collective_id=0, has_side_effects=True, vmem_limit_bytes=48 << 20

time: 75 us -> 70.3 us (0.937)
  Pallas kernels: 71.6 us -> 66.9 us
    pallas_call x1, Pallas kernels: 71.6 us -> 66.9 us  [body(): pl.pallas_call(kernel, out_shape=shapes, in_specs=[hbm] * 5 + [pl.BlockSp...]
where the time goes in v3:
time: 70.3 us; the launch traced here: 70.1 us
  Pallas kernels  66.9 us (95%)
  local copies, waits for them, and re-layouts  1.96 us (3%)
  between operations  1.29 us (2%)
    pallas_call x1, Pallas kernels, body(): pl.pallas_call(kernel, out_shape=shapes, in_specs=[hbm] * 5 + [pl.BlockSp...  66.9 us
    unnamed x3, local copies, waits for them, and re-layouts  1.96 us

profile of v3, /device:TPU:1, one launch (start us, length us, event | category | flops | bytes accessed | tf_op | source)
XLA Modules:
  0.0 70.1 jit_solution(2264574735452171313)
XLA Ops:
  1.3 66.9 %graph_step.1 = (bf16[128,256]{1,0:T(8,128)(2,1)S(1)}, bf16[128,256]{1,0:T(8,128)(2,1)S(1)}, f32[256,256]{1,0:T(8,128)S(1)}) custom-call(bf16[128,256]{1,0:T(8,128)(2,1)} %feat_h.1, bf16[256,256]{1,0:T(8,128)(2,1)} %weight_h.1, bf16[128,256]{1,0:T(8,128)(2,1)} %cot_h.1, bf16[32,128,128]{2,1,0:T(8,128)(2,1)} %bitcast.2, s32[1,32]{1,0:T(1,128)} %bitcast.3, ...), custom_call_target="tpu_custom_call" | custom-call | tf_op jit(solution)/shard_map/graph_step/pallas_call | solution.py:403
  68.2 0.6 copy.13
  68.8 0.6 copy.14
  69.4 0.7 %copy.15 = f32[256,256]{1,0:T(8,128)} copy(f32[256,256]{1,0:T(8,128)S(1)} %get-tuple-element.8) | data formatting | bytes 524288

commit v4 on v3

--- a/solution.py
+++ b/solution.py
@@ -117,7 +117,7 @@
 
     for k in (1, 3):
         send(ca.at[col], ca.at[col], ("cz", k), at("zh", k)[0])
-    for k in (1, 3, 2):
+    for k in (1, 3):
         send(fa.at[row], fa.at[row], ("fz", k), at("zl", k)[0])
     cotangents_on(col, 0)
     features_on(row, 0)
@@ -186,6 +186,7 @@
             block = r4(y + 4 - k) * 8 + r4(zh + 4 - tag) * 2 + c
             send(ca.at[block], ca.at[block], ("cs",), dev(c_=sib))
 
+    send(fa.at[row], fa.at[row], ("fz", 2), at("zl", 2)[0])
     pl.semaphore_wait(near.at[0], 2)
     tell(1, zl_peers)
     across(0)
@@ -365,18 +366,24 @@
         ).astype(BF)
 
     term_xy()
+    tell(4, [dev(c_=sib)])
+    pl.semaphore_wait(near.at[4], 1)
     out_y(2)
-    out_y(3)
-    for g in range(4):
-        grad_x(g)
+    grad_x(0)
     out_z(0)
     term_z()
+    tell(3, [dev(c_=sib)])
+    pl.semaphore_wait(near.at[3], 1)
     out_z(1)
+    out_y(3)
+    grad_x(1)
+    grad_x(2)
+    grad_x(3)
     out_z(2)
+    back_xy()
     grad_z(0)
     grad_z(1)
     grad_z(2)
-    back_xy()
     out_end()
     back_core()
     grad_end()
@@ -384,6 +391,14 @@
 
     for group, ref in enumerate((run.at[pl.ds(0, 23)], run.at[pl.ds(0, 23)], fa.at[pl.ds(0, 2)], w1r, w1r, w1r)):
         sent(ref, group)
+
+
+def hand_over(*refs):
+    copies = [pltpu.make_async_copy(refs[n], refs[n + 3], refs[6].at[n]) for n in range(3)]
+    for copy in copies:
+        copy.start()
+    for copy in copies:
+        copy.wait()
 
 
 def body(features, weight, cotangent, block_index, block_count, block_values):
@@ -400,7 +415,7 @@
         jax.ShapeDtypeStruct((256, 256), F32),
     )
     vmem = pl.BlockSpec(memory_space=pltpu.VMEM)
-    return pl.pallas_call(
+    results = pl.pallas_call(
         kernel,
         out_shape=shapes,
         in_specs=[hbm] * 5 + [pl.BlockSpec(memory_space=pltpu.SMEM)],
@@ -416,13 +431,21 @@
             pltpu.VMEM((16, 16, 128), F32), *(pltpu.VMEM((n, 16, 128), BF) for n in (16, 15, 16, 16, 16)),
             pltpu.SMEM((1, 32), jnp.int32),
             pltpu.SemaphoreType.DMA((6,)), pltpu.SemaphoreType.DMA((KEYS,)),
-            pltpu.SemaphoreType.DMA, pltpu.SemaphoreType.DMA((5,)), pltpu.SemaphoreType.REGULAR((3,)),
+            pltpu.SemaphoreType.DMA, pltpu.SemaphoreType.DMA((5,)), pltpu.SemaphoreType.REGULAR((5,)),
         ],
         compiler_params=pltpu.CompilerParams(
             collective_id=0, has_side_effects=True, vmem_limit_bytes=48 << 20
         ),
         name="graph_step",
     )(*operands, block_count)
+    return pl.pallas_call(
+        hand_over,
+        out_shape=shapes,
+        in_specs=[vmem] * 3,
+        out_specs=(hbm, hbm, hbm),
+        scratch_shapes=[pltpu.SemaphoreType.DMA((3,))],
+        name="hand_over",
+    )(*(pltpu.with_memory_space_constraint(r, pltpu.VMEM) for r in results))
 
 
 def solution(mesh):

time: 70.3 us -> 67.1 us (0.954)
  local copies, waits for them, and re-layouts: 1.96 us -> 0 us
  Pallas kernels: 66.9 us -> 65.7 us
    pallas_call x1, Pallas kernels: 66.9 us -> 64.9 us  [body(): pl.pallas_call(kernel, out_shape=shapes, in_specs=[hbm] * 5 + [pl.BlockSp...]
    unnamed x3 -> x0, local copies, waits for them, and re-layouts: 1.96 us -> none
    pallas_call x0 -> x1, Pallas kernels: none -> 0.77 us  [body(): pl.pallas_call(hand_over, out_shape=shapes, in_specs=[vmem] * 3, out_spec...]
where the time goes in v4:
time: 67.1 us; the launch traced here: 67 us
  Pallas kernels  65.7 us (98%)
  between operations  1.29 us (2%)
    pallas_call x1, Pallas kernels, body(): pl.pallas_call(kernel, out_shape=shapes, in_specs=[hbm] * 5 + [pl.BlockSp...  64.9 us

profile of v4, /device:TPU:1, one launch (start us, length us, event | category | flops | bytes accessed | tf_op | source)
XLA Modules:
  0.0 67.0 jit_solution(3072599629825054540)
XLA Ops:
  1.3 64.9 %graph_step.1 = (bf16[128,256]{1,0:T(8,128)(2,1)S(1)}, bf16[128,256]{1,0:T(8,128)(2,1)S(1)}, f32[256,256]{1,0:T(8,128)S(1)}) custom-call(bf16[128,256]{1,0:T(8,128)(2,1)} %feat_h.1, bf16[256,256]{1,0:T(8,128)(2,1)} %weight_h.1, bf16[128,256]{1,0:T(8,128)(2,1)} %cot_h.1, bf16[32,128,128]{2,1,0:T(8,128)(2,1)} %bitcast.2, s32[1,32]{1,0:T(1,128)} %bitcast.3, ...), custom_call_target="tpu_custom_call" | custom-call | tf_op jit(solution)/shard_map/graph_step/pallas_call | solution.py:418
  66.2 0.8 %hand_over.1 = (bf16[128,256]{1,0:T(8,128)(2,1)}, bf16[128,256]{1,0:T(8,128)(2,1)}, f32[256,256]{1,0:T(8,128)}) custom-call(bf16[128,256]{1,0:T(8,128)(2,1)S(1)} %get-tuple-element.6.refs_0_, bf16[128,256]{1,0:T(8,128)(2,1)S(1)} %get-tuple-element.7.refs_1_, f32[256,256]{1,0:T(8,128)S(1)} %get-tuple-element.8.refs_2_), custom_call_target="tpu_custom_call" | custom-call | tf_op jit(solution)/shard_map/hand_over/pallas_call | solution.py:441

commit v5 on v4

--- a/solution.py
+++ b/solution.py
@@ -228,10 +228,6 @@
     def group(g):
         return r4(zh + ORDER[g])
 
-    for g in range(4):
-        part = pl.ds(sib * 16 + group(g) * 4, 4)
-        send(pout.at[part], rc.at[pl.ds(g * 4, 4)], ("oc", g), dev(c_=sib), 1)
-
     def out_y(g):
         arrive(rc.at[pl.ds(g * 4, 4)], ("oc", g))
         for k in (2, 1, 3):
@@ -242,8 +238,10 @@
         own_y[g] = pout[c * 16 + group(g) * 4 + y].astype(F32) + rc[g * 4 + y].astype(F32)
 
     across(2)
+    for g in range(4):
+        part = pl.ds(sib * 16 + group(g) * 4, 4)
+        send(pout.at[part], rc.at[pl.ds(g * 4, 4)], ("oc", g), dev(c_=sib), 1)
     out_y(0)
-    out_y(1)
 
     def total_y(g):
         total = own_y[g]
@@ -368,6 +366,7 @@
     term_xy()
     tell(4, [dev(c_=sib)])
     pl.semaphore_wait(near.at[4], 1)
+    out_y(1)
     out_y(2)
     grad_x(0)
     out_z(0)

time: 67.1 us -> 66.3 us (0.988)
  Pallas kernels: 65.7 us -> 64.8 us
    pallas_call x1, Pallas kernels: 64.9 us -> 64 us  [body(): pl.pallas_call(kernel, out_shape=shapes, in_specs=[hbm] * 5 + [pl.BlockSp...]
where the time goes in v5:
time: 66.3 us; the launch traced here: 66.1 us
  Pallas kernels  64.8 us (98%)
  between operations  1.29 us (2%)
    pallas_call x1, Pallas kernels, body(): pl.pallas_call(kernel, out_shape=shapes, in_specs=[hbm] * 5 + [pl.BlockSp...  64 us

profile of v5, /device:TPU:1, one launch (start us, length us, event | category | flops | bytes accessed | tf_op | source)
XLA Modules:
  0.0 66.1 jit_solution(1315213617937984799)
XLA Ops:
  1.3 64.0 %graph_step.1 = (bf16[128,256]{1,0:T(8,128)(2,1)S(1)}, bf16[128,256]{1,0:T(8,128)(2,1)S(1)}, f32[256,256]{1,0:T(8,128)S(1)}) custom-call(bf16[128,256]{1,0:T(8,128)(2,1)} %feat_h.1, bf16[256,256]{1,0:T(8,128)(2,1)} %weight_h.1, bf16[128,256]{1,0:T(8,128)(2,1)} %cot_h.1, bf16[32,128,128]{2,1,0:T(8,128)(2,1)} %bitcast.2, s32[1,32]{1,0:T(1,128)} %bitcast.3, ...), custom_call_target="tpu_custom_call" | custom-call | tf_op jit(solution)/shard_map/graph_step/pallas_call | solution.py:417
  65.3 0.8 %hand_over.1 = (bf16[128,256]{1,0:T(8,128)(2,1)}, bf16[128,256]{1,0:T(8,128)(2,1)}, f32[256,256]{1,0:T(8,128)}) custom-call(bf16[128,256]{1,0:T(8,128)(2,1)S(1)} %get-tuple-element.6.refs_0_, bf16[128,256]{1,0:T(8,128)(2,1)S(1)} %get-tuple-element.7.refs_1_, f32[256,256]{1,0:T(8,128)S(1)} %get-tuple-element.8.refs_2_), custom_call_target="tpu_custom_call" | custom-call | tf_op jit(solution)/shard_map/hand_over/pallas_call | solution.py:440
